TPU v7x, 512 devices: a whole 4x4x16 slice. The times are simulated.
512 devices in a mesh: grid: 128 (over z, y, core), band: 4 (over x).
Axes of the slice: x: 4, y: 4, z: 16, core: 2. Of those that a mesh axis runs over, the one named last changes fastest.
Arguments:
- orbitals: bfloat16 [4096, 65536], P(('band', 'grid')), may hold values from -6 to 6
- w_first: bfloat16 [4096, 1024], P(('band', 'grid')), may hold values from -0.09375 to 0.09375
- w_second: bfloat16 [4096, 1024], P(('band', 'grid')), may hold values from -0.09375 to 0.09375
- pivots: int32 [128, 8, 256], P('grid'), may hold values from 0 to 511, as said below
Outputs:
- chosen: bfloat16 [1024, 256], replicated
- quality: float32 [128, 256], P('grid')
Inputs may be any that keep to these rules, and one draw needn't show every extreme that they name: Each list pivots[g, r, :] holds distinct values below 512 and contains 2 * 256 - 1; indices g that agree in all bits from bit r upward have equal lists in round r.
All inputs are finite; a program needn't handle non-finite values.
Results may differ from a plain program's by a relative error of at most 0.0026.
Values may be sent and summed in bfloat16 or wider, within the bound.
A program may use at most 64 MiB of HBM per device.

v0:
```python
import jax
import jax.numpy as jnp
from jax import lax
from jax.sharding import PartitionSpec as P

ridge = 0.1


def partner(block, axis, bit):
    count = lax.axis_size(axis)
    route = []
    for low in range(count):
        high = low | 1 << bit
        if high != low and high < count:
            route += [(low, high), (high, low)]
    return lax.ppermute(block, axis, route)


def log_pivots(chosen):
    count_rows = chosen.shape[0]
    gram_product = lax.dot_general(
        chosen, chosen, (((0,), (0,)), ((), ())), preferred_element_type=jnp.float32
    )
    gram_product = gram_product / count_rows + ridge * jnp.eye(chosen.shape[1], dtype=jnp.float32)
    cholesky_factor = jnp.linalg.cholesky(gram_product)
    return jnp.log(jnp.diagonal(cholesky_factor))


def local(orbitals, w_first, w_second, pivots):
    regrouped = lax.all_to_all(orbitals, "grid", split_axis=1, concat_axis=0, tiled=True)
    contract = (((0,), (0,)), ((), ()))
    whole_first, whole_second = (
        lax.all_gather(w_first, "grid", axis=0, tiled=True),
        lax.all_gather(w_second, "grid", axis=0, tiled=True),
    )
    sketch_first = lax.dot_general(
        whole_first, regrouped, contract, preferred_element_type=jnp.float32
    )
    sketch_second = lax.dot_general(
        whole_second, regrouped, contract, preferred_element_type=jnp.float32
    )
    summed_first, summed_second = lax.psum((sketch_first, sketch_second), "band")
    pair_products = (summed_first * summed_second).astype(jnp.bfloat16)
    order = pivots[0]
    chosen = jnp.take(pair_products, order[0], axis=1)
    quality = log_pivots(chosen)
    sections = lax.axis_size("grid").bit_length() - 1
    for section in range(1, sections + 1):
        partner_cols = partner(chosen, "grid", section - 1)
        upper_flag = lax.axis_index("grid") >> section - 1 & 1 == 1
        lower_set = jnp.where(upper_flag, partner_cols, chosen)
        upper_set = jnp.where(upper_flag, chosen, partner_cols)
        merged = jnp.concatenate([lower_set, upper_set], axis=1)
        chosen = jnp.take(merged, order[section], axis=1)
        quality = quality + log_pivots(chosen)
    return (chosen, quality[None, :])


def solution(mesh):
    in_specs = (
        P(("band", "grid"), None),
        P(("band", "grid"), None),
        P(("band", "grid"), None),
        P("grid", None, None),
    )
    out_specs = (P(), P("grid", None))
    return jax.shard_map(local, mesh=mesh, in_specs=in_specs, out_specs=out_specs, check_vma=False)
```

profile of v0, /device:TPU:1, one launch (start us, length us, event | category | flops | bytes accessed | tf_op | source)
XLA Modules:
  0.0 793.5 jit_solution(10375154173132542540)
XLA Ops:
  7.9 20.6 %all-to-all-start = ((bf16[8,128,512]{2,0,1:T(8,128)(2,1)}), bf16[8,128,512]{2,0,1:T(8,128)(2,1)S(1)}, u32[]{:S(2)}, u32[]{:S(2)}) async-start(bf16[8,128,512]{2,0,1:T(8,128)(2,1)} %bitcast.178), calls=%async_computation | async-start | bytes 2097152 | tf_op jit(solution)/shard_map/all_to_all | solution.py:30
  29.3 129.7 %all-gather.3.cloned.1.call-done = bf16[1024,1024]{1,0:T(8,128)(2,1)} async-done(((bf16[8,1024]{1,0:T(8,128)(2,1)}), bf16[1024,1024]{1,0:T(8,128)(2,1)}) %all-gather.3.cloned.1.call-update) | async-done | bytes 2097168 | tf_op jit(solution)/shard_map/all_gather | solution.py:33
  163.2 136.0 %all-gather.5.cloned.1.call-done = bf16[1024,1024]{1,0:T(8,128)(2,1)} async-done(((bf16[8,1024]{1,0:T(8,128)(2,1)}), bf16[1024,1024]{1,0:T(8,128)(2,1)}) %all-gather.5.cloned.1.call-update) | async-done | bytes 2097168 | tf_op jit(solution)/shard_map/all_gather | solution.py:34
  304.4 103.1 %all-reduce.4.cloned.1.call-done = (f32[1024,512]{1,0:T(8,128)}, f32[1024,512]{1,0:T(8,128)}) async-done(((f32[1024,512]{1,0:T(8,128)}, f32[1024,512]{1,0:T(8,128)}), (f32[1024,512]{1,0:T(8,128)}, f32[1024,512]{1,0:T(8,128)})) %all-reduce.4.cloned.1.call-update) | async-done | bytes 4194320 | tf_op jit(solution)/shard_map/psum | solution.py:42
  415.3 11.7 %cholesky.382 = f32[128,128]{1,0:T(8,128)S(1)} custom-call(f32[128,128]{1,0:T(8,128)S(1)} %cholesky.650), custom_call_target="Cholesky" | custom-call | tf_op jit(solution)/shard_map/jit(cholesky)/cholesky | solution.py:25
  427.1 9.8 %custom-call.31 = f32[1,128,128]{1,2,0:T(8,128)S(1)} custom-call(f32[1,128,128]{2,1,0:T(8,128)S(1)} %get-tuple-element.27), custom_call_target="InvertDiagBlocksLowerTriangular" | custom-call | tf_op jit(solution)/shard_map/jit(cholesky)/cholesky | solution.py:25
  437.4 11.7 %cholesky.399 = f32[128,128]{1,0:T(8,128)S(1)} custom-call(f32[128,128]{1,0:T(8,128)S(1)} %convolution_subtract_fusion.7), custom_call_target="Cholesky" | custom-call | tf_op jit(solution)/shard_map/jit(cholesky)/cholesky | solution.py:25
  459.7 11.7 %cholesky.416 = f32[128,128]{1,0:T(8,128)S(1)} custom-call(f32[128,128]{1,0:T(8,128)S(1)} %cholesky.653), custom_call_target="Cholesky" | custom-call | tf_op jit(solution)/shard_map/jit(cholesky)/cholesky | solution.py:25
  471.5 9.8 %custom-call.32 = f32[1,128,128]{1,2,0:T(8,128)S(1)} custom-call(f32[1,128,128]{2,1,0:T(8,128)S(1)} %get-tuple-element.31), custom_call_target="InvertDiagBlocksLowerTriangular" | custom-call | tf_op jit(solution)/shard_map/jit(cholesky)/cholesky | solution.py:25
  481.8 11.7 %cholesky.433 = f32[128,128]{1,0:T(8,128)S(1)} custom-call(f32[128,128]{1,0:T(8,128)S(1)} %convolution_subtract_fusion.6), custom_call_target="Cholesky" | custom-call | tf_op jit(solution)/shard_map/jit(cholesky)/cholesky | solution.py:25
  505.1 11.7 %cholesky.450 = f32[128,128]{1,0:T(8,128)S(1)} custom-call(f32[128,128]{1,0:T(8,128)S(1)} %cholesky.656), custom_call_target="Cholesky" | custom-call | tf_op jit(solution)/shard_map/jit(cholesky)/cholesky | solution.py:25
  516.9 9.8 %custom-call.33 = f32[1,128,128]{1,2,0:T(8,128)S(1)} custom-call(f32[1,128,128]{2,1,0:T(8,128)S(1)} %get-tuple-element.35), custom_call_target="InvertDiagBlocksLowerTriangular" | custom-call | tf_op jit(solution)/shard_map/jit(cholesky)/cholesky | solution.py:25
  527.2 11.7 %cholesky.467 = f32[128,128]{1,0:T(8,128)S(1)} custom-call(f32[128,128]{1,0:T(8,128)S(1)} %convolution_subtract_fusion.5), custom_call_target="Cholesky" | custom-call | tf_op jit(solution)/shard_map/jit(cholesky)/cholesky | solution.py:25
  549.4 11.7 %cholesky.484 = f32[128,128]{1,0:T(8,128)S(1)} custom-call(f32[128,128]{1,0:T(8,128)S(1)} %cholesky.659), custom_call_target="Cholesky" | custom-call | tf_op jit(solution)/shard_map/jit(cholesky)/cholesky | solution.py:25
  561.1 9.8 %custom-call.34 = f32[1,128,128]{1,2,0:T(8,128)S(1)} custom-call(f32[1,128,128]{2,1,0:T(8,128)S(1)} %get-tuple-element.39), custom_call_target="InvertDiagBlocksLowerTriangular" | custom-call | tf_op jit(solution)/shard_map/jit(cholesky)/cholesky | solution.py:25
  571.4 11.7 %cholesky.501 = f32[128,128]{1,0:T(8,128)S(1)} custom-call(f32[128,128]{1,0:T(8,128)S(1)} %convolution_subtract_fusion.4), custom_call_target="Cholesky" | custom-call | tf_op jit(solution)/shard_map/jit(cholesky)/cholesky | solution.py:25
  594.8 11.7 %cholesky.518 = f32[128,128]{1,0:T(8,128)S(1)} custom-call(f32[128,128]{1,0:T(8,128)S(1)} %cholesky.662), custom_call_target="Cholesky" | custom-call | tf_op jit(solution)/shard_map/jit(cholesky)/cholesky | solution.py:25
  606.6 9.8 %custom-call.35 = f32[1,128,128]{1,2,0:T(8,128)S(1)} custom-call(f32[1,128,128]{2,1,0:T(8,128)S(1)} %get-tuple-element.43), custom_call_target="InvertDiagBlocksLowerTriangular" | custom-call | tf_op jit(solution)/shard_map/jit(cholesky)/cholesky | solution.py:25
  616.9 11.7 %cholesky.535 = f32[128,128]{1,0:T(8,128)S(1)} custom-call(f32[128,128]{1,0:T(8,128)S(1)} %convolution_subtract_fusion.3), custom_call_target="Cholesky" | custom-call | tf_op jit(solution)/shard_map/jit(cholesky)/cholesky | solution.py:25
  635.1 7.5 collective-permute-start.5
  643.2 11.7 %cholesky.552 = f32[128,128]{1,0:T(8,128)S(1)} custom-call(f32[128,128]{1,0:T(8,128)S(1)} %cholesky.665), custom_call_target="Cholesky" | custom-call | tf_op jit(solution)/shard_map/jit(cholesky)/cholesky | solution.py:25
  655.0 9.8 %custom-call.36 = f32[1,128,128]{1,2,0:T(8,128)S(1)} custom-call(f32[1,128,128]{2,1,0:T(8,128)S(1)} %get-tuple-element.47), custom_call_target="InvertDiagBlocksLowerTriangular" | custom-call | tf_op jit(solution)/shard_map/jit(cholesky)/cholesky | solution.py:25
  665.2 11.7 %cholesky.569 = f32[128,128]{1,0:T(8,128)S(1)} custom-call(f32[128,128]{1,0:T(8,128)S(1)} %convolution_subtract_fusion.2), custom_call_target="Cholesky" | custom-call | tf_op jit(solution)/shard_map/jit(cholesky)/cholesky | solution.py:25
  682.0 6.3 collective-permute-done.5
  689.8 9.4 %collective-permute-start.6 = (bf16[1024,256]{0,1:T(8,128)(2,1)S(1)}, bf16[1024,256]{0,1:T(8,128)(2,1)S(1)}, u32[]{:S(2)}, u32[]{:S(2)}) collective-permute-start(bf16[1024,256]{0,1:T(8,128)(2,1)S(1)} %select_bitcast_fusion.1), channel_id=1, source_target_pairs={{0,256},{256,0},{4,260},{260,4},{8,264},{264,8},{12,268},{268,12},... | collective-permute-start | bytes 1572872 | tf_op jit(solution)/shard_map/ppermute | solution.py:16
  699.8 11.7 %cholesky.586 = f32[128,128]{1,0:T(8,128)S(1)} custom-call(f32[128,128]{1,0:T(8,128)S(1)} %cholesky.668), custom_call_target="Cholesky" | custom-call | tf_op jit(solution)/shard_map/jit(cholesky)/cholesky | solution.py:25
  711.6 9.8 %custom-call.37 = f32[1,128,128]{1,2,0:T(8,128)S(1)} custom-call(f32[1,128,128]{2,1,0:T(8,128)S(1)} %get-tuple-element.51), custom_call_target="InvertDiagBlocksLowerTriangular" | custom-call | tf_op jit(solution)/shard_map/jit(cholesky)/cholesky | solution.py:25
  721.8 11.7 %cholesky.603 = f32[128,128]{1,0:T(8,128)S(1)} custom-call(f32[128,128]{1,0:T(8,128)S(1)} %convolution_subtract_fusion.1), custom_call_target="Cholesky" | custom-call | tf_op jit(solution)/shard_map/jit(cholesky)/cholesky | solution.py:25
  738.8 5.2 collective-permute-done.6
  747.0 11.7 %cholesky.620 = f32[128,128]{1,0:T(8,128)S(1)} custom-call(f32[128,128]{1,0:T(8,128)S(1)} %cholesky.671), custom_call_target="Cholesky" | custom-call | tf_op jit(solution)/shard_map/jit(cholesky)/cholesky | solution.py:25
  758.8 9.8 %custom-call.38 = f32[1,128,128]{1,2,0:T(8,128)S(1)} custom-call(f32[1,128,128]{2,1,0:T(8,128)S(1)} %get-tuple-element.55), custom_call_target="InvertDiagBlocksLowerTriangular" | custom-call | tf_op jit(solution)/shard_map/jit(cholesky)/cholesky | solution.py:25
  769.1 11.7 %cholesky.637 = f32[128,128]{1,0:T(8,128)S(1)} custom-call(f32[128,128]{1,0:T(8,128)S(1)} %convolution_subtract_fusion), custom_call_target="Cholesky" | custom-call | tf_op jit(solution)/shard_map/jit(cholesky)/cholesky | solution.py:25
  (181 shorter events, 84.1 us)
Async XLA Ops:
  7.2 151.8 %all-gather.3.cloned.1.call-start = ((), (), s32[]{:S(2)}) async-start(), calls=%async_computation.1 | async-start | bytes 2113536 | tf_op jit(solution)/shard_map/all_gather | solution.py:33
  7.9 151.1 %all-to-all-start = ((bf16[8,128,512]{2,0,1:T(8,128)(2,1)}), bf16[8,128,512]{2,0,1:T(8,128)(2,1)S(1)}, u32[]{:S(2)}, u32[]{:S(2)}) async-start(bf16[8,128,512]{2,0,1:T(8,128)(2,1)} %bitcast.178), calls=%async_computation | async-start | bytes 2097152 | tf_op jit(solution)/shard_map/all_to_all | solution.py:30
  28.5 270.7 %all-gather.5.cloned.1.call-start = ((), (), s32[]{:S(2)}) async-start(), calls=%async_computation.2 | async-start | bytes 2113536 | tf_op jit(solution)/shard_map/all_gather | solution.py:34
  29.2 378.2 %all-reduce.4.cloned.1.call-start = ((), (), s32[]{:S(2)}) async-start(), calls=%async_computation.3 | async-start | bytes 8388608 | tf_op jit(solution)/shard_map/psum | solution.py:42
  303.4 0.7 copy-start
  411.8 42.3 %collective-permute-start = (bf16[1024,256]{0,1:T(8,128)(2,1)S(1)}, bf16[1024,256]{0,1:T(8,128)(2,1)S(1)}, u32[]{:S(2)}, u32[]{:S(2)}) collective-permute-start(bf16[1024,256]{0,1:T(8,128)(2,1)S(1)} %select_bitcast_fusion.7), channel_id=1, source_target_pairs={{0,4},{4,0},{8,12},{12,8},{16,20},{20,16},{24,28},{28,24},{32,36},... | collective-permute-start | bytes 1572872 | tf_op jit(solution)/shard_map/ppermute | solution.py:16
  455.7 42.8 %collective-permute-start.1 = (bf16[1024,256]{0,1:T(8,128)(2,1)S(1)}, bf16[1024,256]{0,1:T(8,128)(2,1)S(1)}, u32[]{:S(2)}, u32[]{:S(2)}) collective-permute-start(bf16[1024,256]{0,1:T(8,128)(2,1)S(1)} %select_bitcast_fusion.6), channel_id=1, source_target_pairs={{0,8},{8,0},{4,12},{12,4},{16,24},{24,16},{20,28},{28,20},{32,40},... | collective-permute-start | bytes 1572872 | tf_op jit(solution)/shard_map/ppermute | solution.py:16
  500.0 43.9 %collective-permute-start.2 = (bf16[1024,256]{0,1:T(8,128)(2,1)S(1)}, bf16[1024,256]{0,1:T(8,128)(2,1)S(1)}, u32[]{:S(2)}, u32[]{:S(2)}) collective-permute-start(bf16[1024,256]{0,1:T(8,128)(2,1)S(1)} %select_bitcast_fusion.5), channel_id=1, source_target_pairs={{0,16},{16,0},{4,20},{20,4},{8,24},{24,8},{12,28},{28,12},{32,48},... | collective-permute-start | bytes 1572872 | tf_op jit(solution)/shard_map/ppermute | solution.py:16
  545.4 42.7 %collective-permute-start.3 = (bf16[1024,256]{0,1:T(8,128)(2,1)S(1)}, bf16[1024,256]{0,1:T(8,128)(2,1)S(1)}, u32[]{:S(2)}, u32[]{:S(2)}) collective-permute-start(bf16[1024,256]{0,1:T(8,128)(2,1)S(1)} %select_bitcast_fusion.4), channel_id=1, source_target_pairs={{0,32},{32,0},{4,36},{36,4},{8,40},{40,8},{12,44},{44,12},{16,48},... | collective-permute-start | bytes 1572872 | tf_op jit(solution)/shard_map/ppermute | solution.py:16
  589.7 43.9 %collective-permute-start.4 = (bf16[1024,256]{0,1:T(8,128)(2,1)S(1)}, bf16[1024,256]{0,1:T(8,128)(2,1)S(1)}, u32[]{:S(2)}, u32[]{:S(2)}) collective-permute-start(bf16[1024,256]{0,1:T(8,128)(2,1)S(1)} %select_bitcast_fusion.3), channel_id=1, source_target_pairs={{0,64},{64,0},{4,68},{68,4},{8,72},{72,8},{12,76},{76,12},{16,80},... | collective-permute-start | bytes 1572872 | tf_op jit(solution)/shard_map/ppermute | solution.py:16
  635.1 53.2 %collective-permute-start.5 = (bf16[1024,256]{0,1:T(8,128)(2,1)S(1)}, bf16[1024,256]{0,1:T(8,128)(2,1)S(1)}, u32[]{:S(2)}, u32[]{:S(2)}) collective-permute-start(bf16[1024,256]{0,1:T(8,128)(2,1)S(1)} %select_bitcast_fusion.2), channel_id=1, source_target_pairs={{0,128},{128,0},{4,132},{132,4},{8,136},{136,8},{12,140},{140,12},... | collective-permute-start | bytes 1572872 | tf_op jit(solution)/shard_map/ppermute | solution.py:16
  689.8 54.2 %collective-permute-start.6 = (bf16[1024,256]{0,1:T(8,128)(2,1)S(1)}, bf16[1024,256]{0,1:T(8,128)(2,1)S(1)}, u32[]{:S(2)}, u32[]{:S(2)}) collective-permute-start(bf16[1024,256]{0,1:T(8,128)(2,1)S(1)} %select_bitcast_fusion.1), channel_id=1, source_target_pairs={{0,256},{256,0},{4,260},{260,4},{8,264},{264,8},{12,268},{268,12},... | collective-permute-start | bytes 1572872 | tf_op jit(solution)/shard_map/ppermute | solution.py:16
Sparse Core Ops, SparseCore 0:
  11.1 147.8 all-gather.2
  162.1 137.0 all-gather.4
  303.5 103.8 all-reduce.3
where the time goes:
time: 799 us; the launch traced here: 793 us
  waiting for transfers between devices  382 us (48%)
  other arithmetic  283 us (35%)
  starting transfers between devices  56.6 us (7%)
  local copies, waits for them, and re-layouts  31.8 us (4%)
  between operations  25.7 us (3%)
  matrix products  14.9 us (2%)
    another operation x56, other arithmetic, log_pivots(): cholesky_factor = jnp.linalg.cholesky(gram_product)  277 us
    all_gather x1, waiting for transfers between devices, local(): lax.all_gather(w_second, 'grid', axis=0, tiled=True)  136 us
    all_gather x1, waiting for transfers between devices, local(): lax.all_gather(w_first, 'grid', axis=0, tiled=True)  130 us
    psum x1, waiting for transfers between devices, local(): lax.psum((sketch_first, sketch_second), 'band')  103 us
    ppermute x7, starting transfers between devices, partner(): return lax.ppermute(block, axis, route)  35.9 us
    all_to_all x1, starting transfers between devices, local(): lax.all_to_all(orbitals, 'grid', split_axis=1, concat_axis=0, tiled=True)  20.6 us
    gather x8, local copies, waits for them, and re-layouts, log_pivots(): return jnp.log(jnp.diagonal(cholesky_factor))  19 us
  transfers between devices with their start and end apart: 11, of which 5 were waited for; matrix products, arithmetic and copies ran while one was open for 34% of the time, Pallas kernels for 0%

commit v1 on v0

v1 whole, which is shorter than its diff:
```python
import jax
import jax.numpy as jnp
from jax import lax
from jax.experimental import pallas as pl
from jax.experimental.pallas import tpu as pltpu
from jax.sharding import PartitionSpec as P

MESH = pl.DeviceIdType.MESH
ridge = 0.1
NZ, NY, NX, NC = 16, 4, 4, 2
ROWS = 8
VM = pltpu.VMEM
DMA = pltpu.SemaphoreType.DMA


def place():
    g = lax.axis_index("grid")
    x = lax.axis_index("band")
    return x, g // 8, (g // 2) % 4, g % 2


def dev(x, z, y, c):
    return (z * 8 + y * 2 + c, x)


def barrier(peers):
    sem = pltpu.get_barrier_semaphore()
    for peer in peers:
        pl.semaphore_signal(sem, inc=1, device_id=peer, device_id_type=MESH)
    pl.semaphore_wait(sem, len(peers))


def send(src, dst, ssem, rsem, peer):
    copy = pltpu.make_async_remote_copy(src, dst, ssem, rsem, device_id=peer, device_id_type=MESH)
    copy.start()
    return copy


def drain(ref, sem):
    pltpu.make_async_copy(ref, ref, sem).wait()


def call(kernel, outs, scratch=(), cid=None, limit=None):
    single = not isinstance(outs, tuple)
    spec = pl.BlockSpec(memory_space=VM)
    params = {}
    if cid is not None:
        params.update(collective_id=cid, has_side_effects=True)
    if limit is not None:
        params.update(vmem_limit_bytes=limit)

    def run(*args):
        return pl.pallas_call(
            kernel,
            out_shape=outs,
            in_specs=[spec] * len(args),
            out_specs=spec if single else tuple(spec for _ in outs),
            scratch_shapes=list(scratch),
            compiler_params=pltpu.CompilerParams(**params),
        )(*args)

    return run


def shape(dims, dtype):
    return jax.ShapeDtypeStruct(dims, dtype)


Z_ORDER = (8, 7, 9, 6, 10, 5, 11, 4, 12, 3, 13, 2, 14, 1, 15)


def own_round(g):
    r = 1
    for bit in range(1, 7):
        r = r + jnp.where(g % (1 << bit) == 0, 1, 0)
    return r


def exchange_kernel(p_ref, wf_ref, ws_ref, ap_ref, wz_ref, pss, prs, qss, qrs, wss, wrs):
    x, z, y, c = place()
    yc = y * 2 + c
    barrier(
        [dev(x, lax.rem(z + d, 16), y, c) for d in range(1, 16)]
        + [dev(x, z, lax.rem(yc + d, 8) // 2, lax.rem(yc + d, 8) % 2) for d in range(1, 8)]
    )
    r = own_round(z * 8 + yc)
    ap_ref[z, yc, 0:1, :] = p_ref[0, 0:1, :]
    ap_ref[z, yc, 1:2, :] = p_ref[0, pl.ds(r, 1), :]
    mine = pl.multiple_of(z * 8, 8)
    wz_ref[pl.ds(mine, 8), 0:1024] = wf_ref[...]
    wz_ref[pl.ds(mine, 8), 1024:2048] = ws_ref[...]
    right, left = dev(x, lax.rem(z + 1, 16), y, c), dev(x, lax.rem(z + 15, 16), y, c)

    def hop(way, step):
        zz = lax.rem(z + 16 - step, 16) if way == 0 else lax.rem(z + step, 16)
        rows = pl.ds(pl.multiple_of(zz * 8, 8), 8)
        return send(
            wz_ref.at[rows], wz_ref.at[rows], wss.at[way, step], wrs.at[way, step], right if way == 0 else left
        )

    sends = []
    for d in Z_ORDER:
        send(ap_ref.at[z, yc], ap_ref.at[z, yc], pss, prs, dev(x, lax.rem(z + d, 16), y, c))
    for step in range(8):
        now = [hop(way, step) for way in (0, 1) if step < 7 or way == 0]
        sends += now
        if step == 2:
            drain(ap_ref.at[0:15, 0], prs)
            drain(ap_ref.at[0:15, 0], pss)
            for d in range(1, 8):
                o = lax.rem(yc + d, 8)
                send(ap_ref.at[:, yc], ap_ref.at[:, yc], qss, qrs, dev(x, z, o // 2, o % 2))
        for copy in now:
            copy.wait_recv()
    for copy in sends:
        copy.wait_send()
    drain(ap_ref.at[:, 0:7], qrs)
    drain(ap_ref.at[:, 0:7], qss)


def select_kernel(ap_ref, orb_ref, sel_ref, cand):
    def pick(parts, row):
        idx = jnp.broadcast_to(row, (8, 128))
        low, seg = idx & 127, idx >> 7
        out = jnp.take_along_axis(parts[0], low, axis=1)
        for s in range(1, 4):
            out = jnp.where(seg == s, jnp.take_along_axis(parts[s], low, axis=1), out)
        return out

    def first(k, _):
        cols = orb_ref[:, pl.ds(pl.multiple_of(k * 512, 512), 512)].astype(jnp.float32)
        parts = [cols[:, 128 * s : 128 * (s + 1)] for s in range(4)]
        t = (k // 8) * 16 + ((k // 2) % 4) * 4 + k % 2
        for h in range(2):
            got = pick(parts, ap_ref[k, 0:1, 128 * h : 128 * (h + 1)])
            cand[k, :, 128 * h : 128 * (h + 1)] = got
            sel_ref[t, :, 128 * h : 128 * (h + 1)] = got.astype(jnp.bfloat16)
        return 0

    sel_ref[2] = jnp.zeros((8, 256), jnp.bfloat16)
    lax.fori_loop(0, 128, first, 0, unroll=4)
    for r in range(1, 8):

        def later(k, _, r=r):
            lower, upper = cand[2 * k], cand[2 * k + 1]
            parts = [lower[:, :128], lower[:, 128:], upper[:, :128], upper[:, 128:]]
            o = k * (1 << r) + (1 << (r - 1))
            t = (o // 8) * 16 + ((o // 2) % 4) * 4 + 2 + o % 2
            got = [pick(parts, ap_ref[o, 1:2, 128 * h : 128 * (h + 1)]) for h in range(2)]
            for h in range(2):
                cand[k, :, 128 * h : 128 * (h + 1)] = got[h]
                sel_ref[t, :, 128 * h : 128 * (h + 1)] = got[h].astype(jnp.bfloat16)
            return 0

        count = 128 >> r
        lax.fori_loop(0, count, later, 0, unroll=min(4, count))


def spread_kernel(sel_ref, wz_ref, got_ref, w_ref, zss, zrs, ss, rs, lsem):
    x, z, y, c = place()
    xr, xl = dev(lax.rem(x + 1, 4), z, y, c), dev(lax.rem(x + 3, 4), z, y, c)
    yr, yl = dev(x, z, lax.rem(y + 1, 4), c), dev(x, z, lax.rem(y + 3, 4), c)
    barrier([dev(x, lax.rem(z + d, 16), y, c) for d in range(1, 16)] + [xr, xl, yr, yl])
    fc, sc = pl.ds(0, 1024), pl.ds(1024, 1024)
    waits = []

    def go(src, dst, i, peer):
        waits.append(send(src, dst, ss.at[i], rs.at[i], peer))
        return waits[-1]

    def unit(yy, xx, cols, rows=slice(None)):
        return w_ref.at[yy, xx, rows, cols]

    a0 = go(wz_ref.at[:, fc], unit(y, x, fc), 0, xr)
    a1 = go(wz_ref.at[:, fc], unit(y, x, fc), 1, xl)
    b0 = go(wz_ref.at[:, sc], unit(y, x, sc), 2, yr)
    b1 = go(wz_ref.at[:, sc], unit(y, x, sc), 3, yl)
    keep = pltpu.make_async_copy(wz_ref, w_ref.at[y, x], lsem.at[0])
    keep.start()
    for d in Z_ORDER:
        t = lax.rem(z + d, 16)
        send(sel_ref.at[t], got_ref.at[z], zss, zrs, dev(x, t, y, c))
    own = pltpu.make_async_copy(sel_ref.at[z], got_ref.at[z], lsem.at[1])
    own.start()
    lo, hi = pl.ds(0, 64), pl.ds(64, 64)
    xm, xp, ym, yp = lax.rem(x + 3, 4), lax.rem(x + 1, 4), lax.rem(y + 3, 4), lax.rem(y + 1, 4)
    a0.wait_recv()
    a2 = go(unit(y, xm, fc, lo), unit(y, xm, fc, lo), 4, xr)
    a1.wait_recv()
    a3 = go(unit(y, xp, fc, hi), unit(y, xp, fc, hi), 5, xl)
    b0.wait_recv()
    b2 = go(unit(ym, x, sc, lo), unit(ym, x, sc, lo), 6, yr)
    b1.wait_recv()
    b3 = go(unit(yp, x, sc, hi), unit(yp, x, sc, hi), 7, yl)
    keep.wait()
    a2.wait_recv()
    a3.wait_recv()
    every, low2, high2 = slice(None), slice(0, 2), slice(2, 4)

    def line(yy, part=every):
        return w_ref.at[yy, part, :, fc]

    def column(xx, part=every):
        return w_ref.at[part, xx, :, sc]

    a4 = go(line(y), line(y), 8, yr)
    a5 = go(line(y), line(y), 9, yl)
    b2.wait_recv()
    b3.wait_recv()
    b4 = go(column(x), column(x), 10, xr)
    b5 = go(column(x), column(x), 11, xl)
    a4.wait_recv()
    a6 = go(line(ym, low2), line(ym, low2), 12, yr)
    a5.wait_recv()
    a7 = go(line(yp, high2), line(yp, high2), 13, yl)
    b4.wait_recv()
    b6 = go(column(xm, low2), column(xm, low2), 14, xr)
    b5.wait_recv()
    b7 = go(column(xp, high2), column(xp, high2), 15, xl)
    for copy in (a6, a7, b6, b7):
        copy.wait_recv()
    for copy in waits:
        copy.wait_send()
    own.wait()
    drain(got_ref.at[0:15], zrs)
    drain(got_ref.at[0:15], zss)


def plane_kernel(r_ref, o_ref, ss, rs, lsem):
    x, z, y, c = place()
    p = y * 4 + x
    barrier([dev(lax.rem(p + d, 16) % 4, z, lax.rem(p + d, 16) // 4, c) for d in range(1, 16)])
    for d in range(1, 16):
        q = lax.rem(p + d, 16)
        send(r_ref.at[:, q], o_ref.at[p], ss, rs, dev(q % 4, z, q // 4, c))
    own = pltpu.make_async_copy(r_ref.at[:, p], o_ref.at[p], lsem)
    own.start()
    own.wait()
    drain(o_ref.at[0:15], rs)
    drain(o_ref.at[0:15], ss)


def sketch_kernel(o_ref, w_ref, s_ref):
    points = o_ref[...].T
    for n in range(0, 2048, 512):
        s_ref[:, n : n + 512] = jnp.dot(points, w_ref[:, n : n + 512], preferred_element_type=jnp.float32)


def swap_kernel(s_ref, o_ref, ss, rs):
    x, z, y, c = place()
    barrier([dev(x, z, y, 1 - c)])
    copy = send(s_ref, o_ref, ss, rs, dev(x, z, y, 1 - c))
    copy.wait()


def pivot_kernel(s_ref, o_ref, logs_ref, cols_ref, gram):
    total = s_ref[...] + o_ref[...]
    points = (total[:, :1024] * total[:, 1024:]).astype(jnp.bfloat16)
    product = lax.dot_general(points, points, (((1,), (1,)), ((), ())), preferred_element_type=jnp.float32)
    row = lax.broadcasted_iota(jnp.int32, (256, 256), 0)
    col = lax.broadcasted_iota(jnp.int32, (256, 256), 1)
    gram[...] = product / 1024 + jnp.where(row == col, ridge, 0.0)
    cols_ref[...] = points.T
    lane = lax.broadcasted_iota(jnp.int32, (8, 128), 1)
    sub = lax.broadcasted_iota(jnp.int32, (8, 128), 0)
    diag = [jnp.ones((8, 128), jnp.float32)] * 2
    for J in range(32):
        base = 8 * J
        halves = (0, 1) if J < 16 else (1,)
        h0 = base // 128
        panel = {h: gram[base : base + 8, 128 * h : 128 * h + 128] for h in halves}
        rows, inv = [], []
        for k in range(8):
            at = base + k - 128 * h0
            coef = jnp.broadcast_to(panel[h0][:, at : at + 1], (8, 128))
            pivot = jnp.broadcast_to(coef[k : k + 1, :], (8, 128))
            scale = 1.0 / pivot
            line = {h: jnp.broadcast_to(panel[h][k : k + 1, :], (8, 128)) for h in halves}
            diag[h0] = jnp.where(lane == at, pivot, diag[h0])
            rows.append({h: line[h] * scale for h in halves})
            factor = jnp.where(sub > k, coef, 0.0)
            panel = {h: panel[h] - factor * rows[k][h] for h in halves}

        def below(i, _, h0=h0, halves=halves, rows=rows, base=base):
            at0 = pl.ds(pl.multiple_of(i * 8, 8), 8)
            tile = {h: gram[at0, 128 * h : 128 * h + 128] for h in halves}
            for k in range(8):
                at = base + k - 128 * h0
                coef = jnp.broadcast_to(tile[h0][:, at : at + 1], (8, 128))
                tile = {h: tile[h] - coef * rows[k][h] for h in halves}
            for h in halves:
                gram[at0, 128 * h : 128 * h + 128] = tile[h]
            return 0

        left = 31 - J
        four = left // 4 * 4
        if four:
            lax.fori_loop(J + 1 + left - four, 32, below, 0, unroll=4)
        for i in range(J + 1, J + 1 + left - four):
            below(i, 0)
    logs_ref[:, 0:128] = 0.5 * jnp.log(diag[0][0:1, :])
    logs_ref[:, 128:256] = 0.5 * jnp.log(diag[1][0:1, :])


def finish_kernel(logs_ref, cols_ref, out_ref, q_ref, near, far, ns, nr, fs, fr, a_s, a_r, b_s, b_r, c_s, c_r, d_s, d_r, lsem):
    x, z, y, c = place()
    p = y * 4 + x
    plane = [dev(lax.rem(p + d, 16) % 4, z, lax.rem(p + d, 16) // 4, c) for d in range(1, 16)]
    deep = [dev(x, lax.rem(z + d, 16), y, c) for d in Z_ORDER]
    twin = dev(x, z, y, 1 - c)
    barrier(plane + deep + [twin])
    root_z, root_p = 8, 2
    is_root = jnp.logical_and(z == root_z, p == root_p)

    @pl.when(is_root)
    def _():
        for d in range(1, 16):
            q = lax.rem(p + d, 16)
            send(cols_ref.at[q, c], out_ref.at[q, c], a_s, a_r, dev(q % 4, z, q // 4, c))
        own = pltpu.make_async_copy(cols_ref.at[p, c], out_ref.at[p, c], lsem)
        own.start()
        own.wait()

    near[p] = logs_ref[...]
    for peer in plane:
        send(near.at[p], near.at[p], ns, nr, peer)

    @pl.when(jnp.logical_and(z == root_z, p != root_p))
    def _():
        drain(out_ref.at[0, 0], a_r)

    @pl.when(z == root_z)
    def _():
        for peer in deep:
            send(out_ref.at[p, c], out_ref.at[p, c], b_s, b_r, peer)

    drain(near.at[0:15], nr)
    drain(near.at[0:15], ns)
    far[z] = near[root_p]
    for peer in deep:
        send(far.at[z], far.at[z], fs, fr, peer)

    @pl.when(z != root_z)
    def _():
        drain(out_ref.at[0, 0], b_r)

    for peer in plane:
        send(out_ref.at[p, c], out_ref.at[p, c], c_s, c_r, peer)
    drain(far.at[0:15], fr)
    drain(far.at[0:15], fs)
    total = near[y * 4 + c]
    g = z * 8 + y * 2 + c
    for r in range(1, 8):
        k = g // (1 << r) * (1 << r) + (1 << (r - 1))
        if r < 4:
            o = k % 8
            total = total + near[(o // 2) * 4 + 2 + o % 2]
        else:
            total = total + far[k // 8]
    q_ref[...] = total
    drain(out_ref.at[0:15, 0], c_r)
    drain(out_ref.at[0:15, 0], c_s)
    last = send(out_ref.at[:, c], out_ref.at[:, c], d_s, d_r, twin)
    last.wait()

    @pl.when(is_root)
    def _():
        drain(out_ref.at[0:15, 0], a_s)

    @pl.when(z == root_z)
    def _():
        drain(out_ref.at[0:15, 0], b_s)


def local(orbitals, w_first, w_second, pivots):
    bf, f32 = jnp.bfloat16, jnp.float32
    lists, wz = call(
        exchange_kernel,
        (shape((16, 8, 2, 256), jnp.int32), shape((128, 2048), bf)),
        [DMA, DMA, DMA, DMA, DMA((2, 8)), DMA((2, 8))],
        cid=1,
    )(pivots, w_first, w_second)
    sel = call(select_kernel, shape((256, 8, 256), bf), [VM((128, 8, 256), f32)])(
        lists.reshape(128, 2, 256), orbitals
    )
    got, w = call(
        spread_kernel,
        (shape((16, 16, 8, 256), bf), shape((4, 4, 128, 2048), bf)),
        [DMA, DMA, DMA((16,)), DMA((16,)), DMA((2,))],
        cid=2,
    )(sel.reshape(16, 16, 8, 256), wz)
    points = call(plane_kernel, shape((16, 16, 8, 256), bf), [DMA, DMA, DMA], cid=3)(got)
    part = call(sketch_kernel, shape((256, 2048), f32))(points.reshape(2048, 256), w.reshape(2048, 2048))
    other = call(swap_kernel, shape((256, 2048), f32), [DMA, DMA], cid=4)(part)
    logs, cols = call(
        pivot_kernel, (shape((1, 256), f32), shape((1024, 256), bf)), [VM((256, 256), f32)]
    )(part, other)
    chosen, quality = call(
        finish_kernel,
        (shape((16, 2, 32, 256), bf), shape((1, 256), f32)),
        [VM((16, 1, 256), f32), VM((16, 1, 256), f32)] + [DMA] * 13,
        cid=5,
    )(logs, cols.reshape(16, 2, 32, 256))
    return chosen.reshape(1024, 256), quality


def solution(mesh):
    in_specs = (
        P(("band", "grid"), None),
        P(("band", "grid"), None),
        P(("band", "grid"), None),
        P("grid", None, None),
    )
    out_specs = (P(), P("grid", None))
    return jax.shard_map(local, mesh=mesh, in_specs=in_specs, out_specs=out_specs, check_vma=False)
```

time: 799 us -> 464 us (0.58)
  Pallas kernels: 0 us -> 460 us
  waiting for transfers between devices: 382 us -> 0 us
  other arithmetic: 283 us -> 0 us
  starting transfers between devices: 56.6 us -> 0 us
  local copies, waits for them, and re-layouts: 31.8 us -> 3.1 us
  between operations: 25.7 us -> 0.67 us
  matrix products: 14.9 us -> 0 us
    pallas_call x0 -> x8, Pallas kernels: none -> 460 us  [run(): pl.pallas_call(kernel, out_shape=outs, in_specs=[spec] * len(args), out_s...]
    another operation x56 -> x0, other arithmetic: 277 us -> none  [log_pivots(): cholesky_factor = jnp.linalg.cholesky(gram_product)]
    all_gather x2 -> x0, waiting for transfers between devices: 266 us -> none  [the longest x1 136 us: local(): lax.all_gather(w_second, 'grid', axis=0, tiled=True)]
    psum x1 -> x0, waiting for transfers between devices: 103 us -> none  [local(): lax.psum((sketch_first, sketch_second), 'band')]
    ppermute x7 -> x0, starting transfers between devices: 35.9 us -> none  [partner(): return lax.ppermute(block, axis, route)]
    gather x16 -> x0, local copies, waits for them, and re-layouts: 28.3 us -> none  [the longest x8 19 us: log_pivots(): return jnp.log(jnp.diagonal(cholesky_factor))]
    all_to_all x1 -> x0, starting transfers between devices: 20.6 us -> none  [local(): lax.all_to_all(orbitals, 'grid', split_axis=1, concat_axis=0, tiled=True)]
    ppermute x7 -> x0, waiting for transfers between devices: 11.5 us -> none  [partner(): return lax.ppermute(block, axis, route)]
  transfers between devices with their start and end apart: 11 -> 0, of which waited for: 5 -> 0; matrix products, arithmetic and copies ran while one was open for 34% -> 0% of each run, Pallas kernels for 0% -> 0%
where the time goes in v1:
time: 464 us
  Pallas kernels  460 us (99%)
    pallas_call x8, Pallas kernels, run(): pl.pallas_call(kernel, out_shape=outs, in_specs=[spec] * len(args), out_s...  460 us

profile of v1, /device:TPU:1, one launch (start us, length us, event | category | flops | bytes accessed | tf_op | source)
XLA Modules:
  0.0 464.0 jit_solution(7592362986255427316)
XLA Ops:
  0.6 39.4 %shard_map.59 = (s32[16,8,2,256]{3,2,1,0:T(2,128)}, bf16[128,2048]{1,0:T(8,128)(2,1)}) custom-call(s32[1,8,256]{2,1,0:T(8,128)} %p_ref.1, bf16[8,1024]{1,0:T(8,128)(2,1)} %wf_ref.1, bf16[8,1024]{1,0:T(8,128)(2,1)} %ws_ref.1), custom_call_target="tpu_custom_call" | custom-call | tf_op jit(solution)/shard_map/pallas_call | solution.py:53
  40.0 16.1 %shard_map.60 = bf16[256,8,256]{2,1,0:T(8,128)(2,1)} custom-call(s32[128,2,256]{2,1,0:T(2,128)} %bitcast.11, bf16[8,65536]{1,0:T(8,128)(2,1)} %orb_ref.1), custom_call_target="tpu_custom_call" | custom-call | tf_op jit(solution)/shard_map/pallas_call | solution.py:53
  56.1 57.0 %shard_map.61 = (bf16[16,16,8,256]{3,2,1,0:T(8,128)(2,1)}, bf16[4,4,128,2048]{3,2,1,0:T(8,128)(2,1)}) custom-call(bf16[16,16,8,256]{3,2,1,0:T(8,128)(2,1)} %bitcast.7, bf16[128,2048]{1,0:T(8,128)(2,1)} %get-tuple-element.11.wz_ref), custom_call_target="tpu_custom_call" | custom-call | tf_op jit(solution)/shard_map/pallas_call | solution.py:53
  113.0 15.1 %shard_map.62 = bf16[16,16,8,256]{3,2,1,0:T(8,128)(2,1)} custom-call(bf16[16,16,8,256]{3,2,1,0:T(8,128)(2,1)} %get-tuple-element.12.r_ref), custom_call_target="tpu_custom_call" | custom-call | tf_op jit(solution)/shard_map/pallas_call | solution.py:53
  128.2 7.4 %shard_map.63.s_ref = f32[256,2048]{1,0:T(8,128)} custom-call(bf16[2048,256]{1,0:T(8,128)(2,1)} %bitcast.8, bf16[2048,2048]{1,0:T(8,128)(2,1)} %bitcast.6), custom_call_target="tpu_custom_call" | custom-call | tf_op jit(solution)/shard_map/pallas_call | solution.py:53
  135.6 13.8 %shard_map.64.o_ref = f32[256,2048]{1,0:T(8,128)} custom-call(f32[256,2048]{1,0:T(8,128)} %shard_map.63.s_ref), custom_call_target="tpu_custom_call" | custom-call | tf_op jit(solution)/shard_map/pallas_call | solution.py:53
  149.4 284.1 %shard_map.65 = (f32[1,256]{1,0:T(1,128)}, bf16[1024,256]{1,0:T(8,128)(2,1)}) custom-call(f32[256,2048]{1,0:T(8,128)} %shard_map.63.s_ref, f32[256,2048]{1,0:T(8,128)} %shard_map.64.o_ref), custom_call_target="tpu_custom_call" | custom-call | tf_op jit(solution)/shard_map/pallas_call | solution.py:53
  433.6 27.3 %shard_map.66 = (bf16[16,2,32,256]{3,2,1,0:T(8,128)(2,1)}, f32[1,256]{1,0:T(1,128)}) custom-call(f32[1,256]{1,0:T(1,128)} %get-tuple-element.14.logs_ref, bf16[16,2,32,256]{3,2,1,0:T(8,128)(2,1)} %bitcast.9), custom_call_target="tpu_custom_call" | custom-call | tf_op jit(solution)/shard_map/pallas_call | solution.py:53
  460.9 1.9 copy.8
  462.8 1.2 copy.9

commit v2 on v1

--- a/solution.py
+++ b/solution.py
@@ -253,7 +253,64 @@
     copy.wait()
 
 
-def pivot_kernel(s_ref, o_ref, logs_ref, cols_ref, gram):
+def splat(row, at):
+    return jnp.broadcast_to(row[:, at:at+1], (8,128))
+
+
+def eliminate(gram, scaled, logs_ref, block=128):
+    lane = lax.broadcasted_iota(jnp.int32, (8, 128), 1)
+    diag = [jnp.ones((8, 128), jnp.float32)] * 2
+    group = block // 8
+    for J in range(32):
+        base = 8 * J
+        halves = (0, 1) if J < 16 else (1,)
+        h0 = base // 128
+        off = base - 128 * h0
+        tile = {h: gram[base:base+8, 128*h:128*h+128] for h in halves}
+        R = [{h: jnp.broadcast_to(tile[h][k:k+1, :], (8,128)) for h in halves} for k in range(8)]
+        e = {(i, j): splat(R[i][h0], off + j) for i in range(8) for j in range(i, 8)}
+        inv = []
+        m = {}
+        for k in range(8):
+            inv.append(1.0 / e[k, k])
+            for i in range(k+1, 8):
+                m[i, k] = e[k, i] * inv[k]
+            for i in range(k+1, 8):
+                for j in range(i, 8):
+                    e[i, j] = e[i, j] - m[i, k] * e[k, j]
+                R[i] = {h: R[i][h] - m[i, k] * R[k][h] for h in halves}
+            diag[h0] = jnp.where(lane == off + k, e[k, k], diag[h0])
+        X = [{h: R[k][h] * inv[k] for h in halves} for k in range(8)]
+        sub = lax.broadcasted_iota(jnp.int32, (8, 128), 0)
+        for h in halves:
+            u, s = R[0][h], X[0][h]
+            for k in range(1, 8):
+                u = jnp.where(sub == k, R[k][h], u)
+                s = jnp.where(sub == k, X[k][h], s)
+            gram[base:base+8, 128*h:128*h+128] = u
+            scaled[base:base+8, 128*h:128*h+128] = s
+        last = (J // group + 1) * group
+        for i in range(J+1, last):
+            t = {h: gram[8*i:8*i+8, 128*h:128*h+128] for h in halves}
+            C = [splat(t[h0], off + k) for k in range(8)]
+            for k in range(8):
+                for q in range(k+1, 8):
+                    C[q] = C[q] - C[k] * m[q, k]
+            for h in halves:
+                acc = t[h]
+                for k in range(8):
+                    acc = acc - C[k] * X[k][h]
+                gram[8*i:8*i+8, 128*h:128*h+128] = acc
+        if J % group == group-1 and J < 31:
+            r0 = base + 8; p0 = r0 - block; c0 = r0 // 128 * 128
+            upd = lax.dot_general(gram[p0:r0, r0//128*128:], scaled[p0:r0, c0:], (((0,),(0,)),((),())), precision=lax.Precision.HIGHEST, preferred_element_type=jnp.float32)
+            cut = r0 - r0//128*128
+            gram[r0:, c0:] = gram[r0:, c0:] - upd[cut:]
+    logs_ref[:, 0:128] = 0.5 * jnp.log(diag[0][0:1, :])
+    logs_ref[:, 128:256] = 0.5 * jnp.log(diag[1][0:1, :])
+
+
+def pivot_kernel(s_ref, o_ref, logs_ref, cols_ref, gram, scaled):
     total = s_ref[...] + o_ref[...]
     points = (total[:, :1024] * total[:, 1024:]).astype(jnp.bfloat16)
     product = lax.dot_general(points, points, (((1,), (1,)), ((), ())), preferred_element_type=jnp.float32)
@@ -261,45 +318,7 @@
     col = lax.broadcasted_iota(jnp.int32, (256, 256), 1)
     gram[...] = product / 1024 + jnp.where(row == col, ridge, 0.0)
     cols_ref[...] = points.T
-    lane = lax.broadcasted_iota(jnp.int32, (8, 128), 1)
-    sub = lax.broadcasted_iota(jnp.int32, (8, 128), 0)
-    diag = [jnp.ones((8, 128), jnp.float32)] * 2
-    for J in range(32):
-        base = 8 * J
-        halves = (0, 1) if J < 16 else (1,)
-        h0 = base // 128
-        panel = {h: gram[base : base + 8, 128 * h : 128 * h + 128] for h in halves}
-        rows, inv = [], []
-        for k in range(8):
-            at = base + k - 128 * h0
-            coef = jnp.broadcast_to(panel[h0][:, at : at + 1], (8, 128))
-            pivot = jnp.broadcast_to(coef[k : k + 1, :], (8, 128))
-            scale = 1.0 / pivot
-            line = {h: jnp.broadcast_to(panel[h][k : k + 1, :], (8, 128)) for h in halves}
-            diag[h0] = jnp.where(lane == at, pivot, diag[h0])
-            rows.append({h: line[h] * scale for h in halves})
-            factor = jnp.where(sub > k, coef, 0.0)
-            panel = {h: panel[h] - factor * rows[k][h] for h in halves}
-
-        def below(i, _, h0=h0, halves=halves, rows=rows, base=base):
-            at0 = pl.ds(pl.multiple_of(i * 8, 8), 8)
-            tile = {h: gram[at0, 128 * h : 128 * h + 128] for h in halves}
-            for k in range(8):
-                at = base + k - 128 * h0
-                coef = jnp.broadcast_to(tile[h0][:, at : at + 1], (8, 128))
-                tile = {h: tile[h] - coef * rows[k][h] for h in halves}
-            for h in halves:
-                gram[at0, 128 * h : 128 * h + 128] = tile[h]
-            return 0
-
-        left = 31 - J
-        four = left // 4 * 4
-        if four:
-            lax.fori_loop(J + 1 + left - four, 32, below, 0, unroll=4)
-        for i in range(J + 1, J + 1 + left - four):
-            below(i, 0)
-    logs_ref[:, 0:128] = 0.5 * jnp.log(diag[0][0:1, :])
-    logs_ref[:, 128:256] = 0.5 * jnp.log(diag[1][0:1, :])
+    eliminate(gram, scaled, logs_ref)
 
 
 def finish_kernel(logs_ref, cols_ref, out_ref, q_ref, near, far, ns, nr, fs, fr, a_s, a_r, b_s, b_r, c_s, c_r, d_s, d_r, lsem):
@@ -393,7 +412,7 @@
     part = call(sketch_kernel, shape((256, 2048), f32))(points.reshape(2048, 256), w.reshape(2048, 2048))
     other = call(swap_kernel, shape((256, 2048), f32), [DMA, DMA], cid=4)(part)
     logs, cols = call(
-        pivot_kernel, (shape((1, 256), f32), shape((1024, 256), bf)), [VM((256, 256), f32)]
+        pivot_kernel, (shape((1, 256), f32), shape((1024, 256), bf)), [VM((256, 256), f32)] * 2
     )(part, other)
     chosen, quality = call(
         finish_kernel,

time: 464 us -> 192 us (0.41)
  Pallas kernels: 460 us -> 187 us
    pallas_call x8, Pallas kernels: 460 us -> 187 us  [run(): pl.pallas_call(kernel, out_shape=outs, in_specs=[spec] * len(args), out_s...]
where the time goes in v2:
time: 192 us; the launch traced here: 191 us
  Pallas kernels  187 us (97%)
  local copies, waits for them, and re-layouts  3.1 us (2%)
    pallas_call x8, Pallas kernels, run(): pl.pallas_call(kernel, out_shape=outs, in_specs=[spec] * len(args), out_s...  187 us

profile of v2, /device:TPU:1, one launch (start us, length us, event | category | flops | bytes accessed | tf_op | source)
XLA Modules:
  0.0 191.2 jit_solution(14290760020927777515)
XLA Ops:
  0.6 39.4 %shard_map.59 = (s32[16,8,2,256]{3,2,1,0:T(2,128)}, bf16[128,2048]{1,0:T(8,128)(2,1)}) custom-call(s32[1,8,256]{2,1,0:T(8,128)} %p_ref.1, bf16[8,1024]{1,0:T(8,128)(2,1)} %wf_ref.1, bf16[8,1024]{1,0:T(8,128)(2,1)} %ws_ref.1), custom_call_target="tpu_custom_call" | custom-call | tf_op jit(solution)/shard_map/pallas_call | solution.py:53
  40.0 16.1 %shard_map.60 = bf16[256,8,256]{2,1,0:T(8,128)(2,1)} custom-call(s32[128,2,256]{2,1,0:T(2,128)} %bitcast.11, bf16[8,65536]{1,0:T(8,128)(2,1)} %orb_ref.1), custom_call_target="tpu_custom_call" | custom-call | tf_op jit(solution)/shard_map/pallas_call | solution.py:53
  56.1 57.0 %shard_map.61 = (bf16[16,16,8,256]{3,2,1,0:T(8,128)(2,1)}, bf16[4,4,128,2048]{3,2,1,0:T(8,128)(2,1)}) custom-call(bf16[16,16,8,256]{3,2,1,0:T(8,128)(2,1)} %bitcast.7, bf16[128,2048]{1,0:T(8,128)(2,1)} %get-tuple-element.11.wz_ref), custom_call_target="tpu_custom_call" | custom-call | tf_op jit(solution)/shard_map/pallas_call | solution.py:53
  113.0 15.1 %shard_map.62 = bf16[16,16,8,256]{3,2,1,0:T(8,128)(2,1)} custom-call(bf16[16,16,8,256]{3,2,1,0:T(8,128)(2,1)} %get-tuple-element.12.r_ref), custom_call_target="tpu_custom_call" | custom-call | tf_op jit(solution)/shard_map/pallas_call | solution.py:53
  128.2 7.4 %shard_map.63.s_ref = f32[256,2048]{1,0:T(8,128)} custom-call(bf16[2048,256]{1,0:T(8,128)(2,1)} %bitcast.8, bf16[2048,2048]{1,0:T(8,128)(2,1)} %bitcast.6), custom_call_target="tpu_custom_call" | custom-call | tf_op jit(solution)/shard_map/pallas_call | solution.py:53
  135.6 13.8 %shard_map.64.o_ref = f32[256,2048]{1,0:T(8,128)} custom-call(f32[256,2048]{1,0:T(8,128)} %shard_map.63.s_ref), custom_call_target="tpu_custom_call" | custom-call | tf_op jit(solution)/shard_map/pallas_call | solution.py:53
  149.4 11.3 %shard_map.65 = (f32[1,256]{1,0:T(1,128)}, bf16[1024,256]{1,0:T(8,128)(2,1)}) custom-call(f32[256,2048]{1,0:T(8,128)} %shard_map.63.s_ref, f32[256,2048]{1,0:T(8,128)} %shard_map.64.o_ref), custom_call_target="tpu_custom_call" | custom-call | tf_op jit(solution)/shard_map/pallas_call | solution.py:53
  160.7 27.3 %shard_map.66 = (bf16[16,2,32,256]{3,2,1,0:T(8,128)(2,1)}, f32[1,256]{1,0:T(1,128)}) custom-call(f32[1,256]{1,0:T(1,128)} %get-tuple-element.14.logs_ref, bf16[16,2,32,256]{3,2,1,0:T(8,128)(2,1)} %bitcast.9), custom_call_target="tpu_custom_call" | custom-call | tf_op jit(solution)/shard_map/pallas_call | solution.py:53
  188.1 1.9 copy.8
  189.9 1.2 copy.9
